TPU v7x, 256 devices: a whole 4x4x8 slice. The times are simulated.
256 devices in a mesh: prow: 8 (over z_lo, y), pcol: 32 (over z_hi, x, core).
Axes of the slice: x: 4, y: 4, z: 8 (z_hi: 4, z_lo: 2; z = z_hi * 2 + z_lo), core: 2. Of those that a mesh axis runs over, the one named last changes fastest.
Arguments:
- ancestor_inverse: bfloat16 [24576, 24576], P('prow', 'pcol'), may hold values from -6 to 6
- tile_pattern: int32 [64, 64], replicated, may hold values 0 or 1
- rows_first: int32 [24576], replicated, may hold values 0 or 1
- rows_second: int32 [24576], replicated, may hold values 0 or 1
- panel_first: bfloat16 [24576, 512], P('prow', 'pcol'), may hold values from -0.0390625 to 0.0390625
- panel_second: bfloat16 [24576, 512], P('prow', 'pcol'), may hold values from -0.21875 to 0.21875
- inner_panel: bfloat16 [512, 512], replicated, may hold values from -0.25 to 0.25
- pivot_first: float32 [512, 512], replicated, may hold values from -6 to 6
- pivot_second: float32 [512, 512], replicated, may hold values from -6 to 6
Outputs:
- column_first: bfloat16 [24576, 512], P(('prow', 'pcol'))
- diagonal_first: float32 [512, 512], replicated
- inner_second: float32 [512, 512], replicated
- column_second: bfloat16 [24576, 512], P(('prow', 'pcol'))
- diagonal_second: float32 [512, 512], replicated
Inputs may be any that keep to these rules, and one draw needn't show every extreme that they name: `tile_pattern`: 1 marks a structurally nonzero tile. `rows_first`: 1 marks a row of the first supernode's structure. By construction here, a row belongs to the second supernode's structure only where both rows_second and rows_first are 1.
All inputs are finite; a program needn't handle non-finite values.
Results may differ from a plain program's by a relative error of at most 0.015.
Values may be sent and summed in bfloat16 or wider, within the bound.
A program may use at most 128 MiB of HBM per device.

v0:
```python
import jax
import jax.numpy as jnp
from jax import lax
from jax.sharding import PartitionSpec as P

TILE = 384


def from_root(shard, axis, root):
    mine = lax.axis_index(axis) == root
    return lax.psum(jnp.where(mine, shard, jnp.zeros_like(shard)), axis)


def mask_tiles(block, pattern, row_start, col_start):
    tile_rows = block.shape[0] // TILE
    tile_cols = block.shape[1] // TILE
    window = lax.dynamic_slice(pattern, (row_start, col_start), (tile_rows, tile_cols)).astype(
        jnp.bfloat16
    )
    shaped = block.reshape(tile_rows, TILE, tile_cols, TILE) * window[:, None, :, None]
    return shaped.reshape(block.shape)


def body(
    ancestor_inverse,
    tile_pattern,
    rows_first,
    rows_second,
    panel_first,
    panel_second,
    inner_panel,
    pivot_first,
    pivot_second,
):
    row_count = lax.axis_size("prow")
    col_count = lax.axis_size("pcol")
    row_id = lax.axis_index("prow")
    col_id = lax.axis_index("pcol")
    row_block = ancestor_inverse.shape[0]
    col_block = ancestor_inverse.shape[1]
    share = row_block // col_count
    sparse = mask_tiles(
        ancestor_inverse, tile_pattern, row_id * (row_block // TILE), col_id * (col_block // TILE)
    )
    struct_first = lax.dynamic_slice_in_dim(rows_first, row_id * row_block, row_block).astype(
        jnp.bfloat16
    )
    struct_second = struct_first * lax.dynamic_slice_in_dim(
        rows_second, row_id * row_block, row_block
    ).astype(jnp.bfloat16)
    local_first = panel_first * struct_first[:, None]
    local_second = panel_second * struct_second[:, None]
    source = col_id * row_count // col_count
    offset = col_id * col_block - source * row_block

    def summed_terms(columns):
        return jnp.dot(sparse, columns, preferred_element_type=jnp.float32)

    def ancestor_terms(local):
        full = lax.all_gather(local, "pcol", axis=1, tiled=True)
        mirrored = from_root(lax.dynamic_slice_in_dim(full, offset, col_block, 0), "prow", source)
        return (
            full,
            lax.psum_scatter(
                summed_terms(mirrored).astype(jnp.bfloat16), "pcol", scatter_dimension=0, tiled=True
            ).astype(jnp.float32),
        )

    full_first, sum_first = ancestor_terms(local_first)
    full_second, sum_second = ancestor_terms(local_second)
    column_first = (-sum_first).astype(jnp.bfloat16)
    own_first = lax.dynamic_slice_in_dim(full_first, col_id * share, share, 0)
    own_second = lax.dynamic_slice_in_dim(full_second, col_id * share, share, 0)
    corr_first, crossed = lax.psum(
        (
            jnp.dot(own_first.T, column_first, preferred_element_type=jnp.float32),
            jnp.dot(column_first.T, own_second, preferred_element_type=jnp.float32),
        ),
        ("prow", "pcol"),
    )
    diagonal_first = pivot_first - corr_first
    column_second = (
        -(sum_second + jnp.dot(column_first, inner_panel, preferred_element_type=jnp.float32))
    ).astype(jnp.bfloat16)
    inner_wide = inner_panel.astype(jnp.float32)
    inner_second = -(jnp.dot(diagonal_first, inner_wide, precision=lax.Precision.HIGHEST) + crossed)
    corr_second = lax.psum(
        jnp.dot(own_second.T, column_second, preferred_element_type=jnp.float32), ("prow", "pcol")
    )
    diagonal_second = (
        pivot_second
        - jnp.dot(inner_wide.T, inner_second, precision=lax.Precision.HIGHEST)
        - corr_second
    )
    return (column_first, diagonal_first, inner_second, column_second, diagonal_second)


def solution(mesh):
    return jax.shard_map(
        body,
        mesh=mesh,
        in_specs=(
            P("prow", "pcol"),
            P(),
            P(),
            P(),
            P("prow", "pcol"),
            P("prow", "pcol"),
            P(),
            P(),
            P(),
        ),
        out_specs=(P(("prow", "pcol"), None), P(), P(), P(("prow", "pcol"), None), P()),
        check_vma=False,
    )
```

profile of v0, /device:TPU:8, one launch (start us, length us, event | category | flops | bytes accessed | tf_op | source)
XLA Modules:
  0.0 701.2 jit_solution(2915164507721282915)
XLA Ops:
  7.2 0.0 copy-start
  7.2 0.0 all-gather.5.cloned.1.call-start
  7.2 0.8 fusion.13
  8.0 1.5 broadcast_multiply_fusion
  9.6 0.0 all-gather.5.cloned.1.call-update
  9.6 0.0 all-gather.3.cloned.1.call-start
  9.6 1.5 broadcast_multiply_fusion.1
  11.2 0.0 all-gather.3.cloned.1.call-update
  11.2 0.0 all-reduce.7.cloned.1.call-start
  11.3 59.7 %all-gather.5.cloned.1.call-done = bf16[3072,512]{0,1:T(8,128)(2,1)} async-done(((bf16[3072,16]{0,1:T(8,128)(2,1)}), bf16[3072,512]{0,1:T(8,128)(2,1)}) %all-gather.5.cloned.1.call-update) | async-done | bytes 3145744 | tf_op jit(solution)/shard_map/all_gather | solution.py:60
  71.0 2.1 dynamic-slice_select_fusion
  73.2 55.8 %all-gather.3.cloned.1.call-done = bf16[3072,512]{0,1:T(8,128)(2,1)} async-done(((bf16[3072,16]{0,1:T(8,128)(2,1)}), bf16[3072,512]{0,1:T(8,128)(2,1)}) %all-gather.3.cloned.1.call-update) | async-done | bytes 3145744 | tf_op jit(solution)/shard_map/all_gather | solution.py:60
  129.0 2.1 dynamic-slice_select_fusion.1
  131.1 0.0 all-reduce.7.cloned.1.call-update
  131.2 0.0 reduce-scatter.3.cloned.1.call-start
  131.2 0.8 dynamic-slice_convert_fusion.2
  132.0 2.5 mul.55
  134.5 3.0 copy.18
  137.5 76.0 %all-reduce.7.cloned.1.call-done = (bf16[768,512]{0,1:T(8,128)(2,1)}, bf16[768,512]{0,1:T(8,128)(2,1)}) async-done(((bf16[768,512]{0,1:T(8,128)(2,1)}, bf16[768,512]{0,1:T(8,128)(2,1)}), (bf16[768,512]{0,1:T(8,128)(2,1)}, bf16[768,512]{0,1:T(8,128)(2,1)})) %all-reduce.7.cloned.1.call-update) | async-done | bytes 1572880 | tf_op jit(solution)/shard_map/psum | solution.py:11
  213.4 0.0 copy-start.9
  213.4 8.4 %convolution_convert_fusion.1 = bf16[3072,512]{1,0:T(8,128)(2,1)} fusion(bf16[768,512]{0,1:T(8,128)(2,1)} %get-tuple-element.13, bf16[3072,768]{1,0:T(8,128)(2,1)} %param.9, bf16[3072,768]{1,0:T(8,128)(2,1)} %bitcast.21), kind=kOutput, calls=%fused_computation.1 | convolution fusion | flops 2419851264 | bytes 13369344 | tf_op jit(solution)/shard_map/dot_general | solution.py:57
  221.8 0.0 reduce-scatter.3.cloned.1.call-update
  221.8 0.0 reduce-scatter.5.cloned.1.call-start
  221.9 0.0 copy-done.9
  221.9 7.9 %convolution_convert_fusion = bf16[3072,512]{1,0:T(8,128)(2,1)} fusion(bf16[768,512]{0,1:T(8,128)(2,1)S(1)} %copy-done.9, bf16[3072,768]{1,0:T(8,128)(2,1)} %param.9, bf16[3072,768]{1,0:T(8,128)(2,1)} %bitcast.22), kind=kOutput, calls=%fused_computation | convolution fusion | flops 2419851264 | bytes 13369344 | tf_op jit(solution)/shard_map/dot_general | solution.py:57
  229.8 0.0 reduce-scatter.5.cloned.1.call-update
  229.8 0.0 copy-start.6
  229.8 0.2 all-reduce.5.cloned.1.call-start
  230.0 88.8 %reduce-scatter.3.cloned.1.call-done = bf16[96,512]{1,0:T(8,128)(2,1)} async-done(((bf16[3072,512]{1,0:T(8,128)(2,1)}), bf16[96,512]{1,0:T(8,128)(2,1)}) %reduce-scatter.3.cloned.1.call-update) | async-done | bytes 98320 | tf_op jit(solution)/shard_map/reduce_scatter | solution.py:64
  318.8 0.9 negate_convert_fusion
  319.8 0.0 copy-start.4
  319.8 0.0 copy-start.5
  319.8 2.4 fusion.11
  322.2 2.3 fusion.7
  324.4 91.8 %reduce-scatter.5.cloned.1.call-done = bf16[96,512]{1,0:T(8,128)(2,1)} async-done(((bf16[3072,512]{1,0:T(8,128)(2,1)}), bf16[96,512]{1,0:T(8,128)(2,1)}) %reduce-scatter.5.cloned.1.call-update) | async-done | bytes 98320 | tf_op jit(solution)/shard_map/reduce_scatter | solution.py:64
  416.3 0.0 copy-done
  416.3 1.1 fusion.6
  417.4 0.0 copy-start.8
  417.4 2.4 fusion.9
  419.8 0.0 all-reduce.5.cloned.1.call-update
  419.8 0.0 copy-done.6
  419.8 1.3 copy.14
  421.1 0.0 copy-done.4
  421.1 264.4 %all-reduce.5.cloned.1.call-done = (f32[512,512]{1,0:T(8,128)}, f32[512,512]{1,0:T(8,128)}, f32[512,512]{0,1:T(8,128)}) async-done(((f32[512,512]{1,0:T(8,128)}, f32[512,512]{1,0:T(8,128)}, f32[512,512]{0,1:T(8,128)}), (f32[512,512]{1,0:T(8,128)}, f32[512,512]{1,0:T(8,128)}, f32[512,512]{0,1:T(8,128)})) %all-reduce.5.cloned.1.call-update) | async-done | bytes 3145744 | tf_op jit(solution)/shard_map/psum | solution.py:74
  685.6 0.0 copy-start.3
  685.6 0.0 copy-start.7
  685.6 0.0 copy-done.5
  685.6 1.6 sub.18
  687.2 0.0 copy-done.8
  687.2 0.0 copy-start.1
  687.2 2.6 fusion.2
  689.8 0.0 copy-start.2
  689.8 0.0 copy-done.3
  689.8 0.0 copy-done.7
  689.8 2.0 fusion.4
  691.8 2.5 copy.16
  694.4 0.0 copy-done.1
  694.4 0.0 copy-done.2
Async XLA Ops:
  7.2 409.1 %copy-start = (bf16[512,512]{1,0:T(8,128)(2,1)S(1)}, bf16[512,512]{1,0:T(8,128)(2,1)}, u32[]{:S(2)}) copy-start(bf16[512,512]{1,0:T(8,128)(2,1)} %param.15) | copy-start | bytes 1572868
  7.2 63.8 %all-gather.5.cloned.1.call-start = ((), (), s32[]{:S(2)}) async-start(), calls=%async_computation.4 | async-start | bytes 3244032 | tf_op jit(solution)/shard_map/all_gather | solution.py:60
  9.6 119.4 %all-gather.3.cloned.1.call-start = ((), (), s32[]{:S(2)}) async-start(), calls=%async_computation.2 | async-start | bytes 3244032 | tf_op jit(solution)/shard_map/all_gather | solution.py:60
  11.2 202.2 %all-reduce.7.cloned.1.call-start = ((), (), s32[]{:S(2)}) async-start(), calls=%async_computation.7 | async-start | bytes 3145728 | tf_op jit(solution)/shard_map/psum | solution.py:11
  131.2 187.7 %reduce-scatter.3.cloned.1.call-start = ((), (), s32[]{:S(2)}) async-start(), calls=%async_computation.3 | async-start | bytes 3244032 | tf_op jit(solution)/shard_map/reduce_scatter | solution.py:64
  213.4 8.4 %copy-start.9 = (bf16[768,512]{0,1:T(8,128)(2,1)S(1)}, bf16[768,512]{0,1:T(8,128)(2,1)}, u32[]{:S(2)}) copy-start(bf16[768,512]{0,1:T(8,128)(2,1)} %get-tuple-element.14) | copy-start | bytes 2359300
  221.8 194.4 %reduce-scatter.5.cloned.1.call-start = ((), (), s32[]{:S(2)}) async-start(), calls=%async_computation.5 | async-start | bytes 3244032 | tf_op jit(solution)/shard_map/reduce_scatter | solution.py:64
  229.8 190.0 %copy-start.6 = (f32[512,512]{1,0:T(8,128)S(1)}, f32[512,512]{1,0:T(8,128)}, u32[]{:S(2)}) copy-start(f32[512,512]{1,0:T(8,128)} %param.17) | copy-start | bytes 3145732
  229.8 455.8 %all-reduce.5.cloned.1.call-start = ((), (), s32[]{:S(2)}) async-start(), calls=%async_computation.6 | async-start | bytes 6291456 | tf_op jit(solution)/shard_map/psum | solution.py:74
  319.8 101.4 %copy-start.4 = (bf16[96,512]{1,0:T(8,128)(2,1)}, bf16[96,512]{1,0:T(8,128)(2,1)S(1)}, u32[]{:S(2)}) copy-start(bf16[96,512]{1,0:T(8,128)(2,1)S(1)} %negate_convert_fusion) | copy-start | bytes 294916
  319.8 365.8 %copy-start.5 = (f32[512,512]{1,0:T(8,128)S(1)}, f32[512,512]{1,0:T(8,128)}, u32[]{:S(2)}) copy-start(f32[512,512]{1,0:T(8,128)} %param.16) | copy-start | bytes 3145732
  417.4 269.8 %copy-start.8 = (bf16[96,512]{1,0:T(8,128)(2,1)}, bf16[96,512]{1,0:T(8,128)(2,1)S(1)}, u32[]{:S(2)}) copy-start(bf16[96,512]{1,0:T(8,128)(2,1)S(1)} %fusion.6) | copy-start | bytes 294916
  685.6 4.2 copy-start.3
  685.6 4.2 copy-start.7
  687.2 7.2 %copy-start.1 = (f32[512,512]{1,0:T(8,128)}, f32[512,512]{1,0:T(8,128)S(1)}, u32[]{:S(2)}) copy-start(f32[512,512]{1,0:T(8,128)S(1)} %sub.18) | copy-start | bytes 3145732
  689.8 4.6 copy-start.2
Sparse Core Ops, SparseCore 0:
  11.1 59.8 all-gather.4
  74.1 54.8 all-gather.2
  132.3 81.1 all-reduce.6
  222.0 96.8 reduce-scatter.2
  323.1 93.1 reduce-scatter.4
  422.5 263.0 all-reduce.4
where the time goes:
time: 702 us; the launch traced here: 701 us
  waiting for transfers between devices  637 us (91%)
  matrix products  29 us (4%)
  between operations  14.3 us (2%)
  other arithmetic  11.4 us (2%)
  local copies, waits for them, and re-layouts  9.39 us (1%)
    psum x1, waiting for transfers between devices, body(): lax.psum((jnp.dot(own_first.T, column_first, preferred_element_type=jnp.f...  264 us
    reduce_scatter x2, waiting for transfers between devices, ancestor_terms(): lax.psum_scatter(summed_terms(mirrored).astype(jnp.bfloat16), 'pcol', sca...  181 us
    all_gather x2, waiting for transfers between devices, ancestor_terms(): full = lax.all_gather(local, 'pcol', axis=1, tiled=True)  116 us
    psum x1, waiting for transfers between devices, from_root(): return lax.psum(jnp.where(mine, shard, jnp.zeros_like(shard)), axis)  76 us
    dot_general x2, matrix products, summed_terms(): return jnp.dot(sparse, columns, preferred_element_type=jnp.float32)  16.2 us
  transfers between devices with their start and end apart: 6, of which 6 were waited for; matrix products, arithmetic and copies ran while one was open for 4% of the time, Pallas kernels for 0%

commit v1 on v0

--- a/solution.py
+++ b/solution.py
@@ -8,7 +8,7 @@
 
 def from_root(shard, axis, root):
     mine = lax.axis_index(axis) == root
-    return lax.psum(jnp.where(mine, shard, jnp.zeros_like(shard)), axis)
+    return jnp.sum(lax.all_gather(jnp.where(mine, shard, jnp.zeros_like(shard)), axis), axis=0)
 
 
 def mask_tiles(block, pattern, row_start, col_start):

time: 702 us -> 761 us (1.084)
  waiting for transfers between devices: 637 us -> 682 us
  local copies, waits for them, and re-layouts: 9.39 us -> 19.2 us
  other arithmetic: 11.4 us -> 20.7 us
    all_gather x0 -> x2, waiting for transfers between devices: none -> 126 us  [from_root(): lax.all_gather(jnp.where(mine, shard, jnp.zeros_like(shard)), axis)]
    psum x1 -> x0, waiting for transfers between devices: 76 us -> none  [from_root(): return lax.psum(jnp.where(mine, shard, jnp.zeros_like(shard)), axis)]
    unnamed x23 -> x33, local copies, waits for them, and re-layouts: 6.89 us -> 16.7 us
    reduce_sum x0 -> x2, other arithmetic: none -> 9.26 us  [from_root(): jnp.sum(lax.all_gather(jnp.where(mine, shard, jnp.zeros_like(shard)), axi...]
  transfers between devices with their start and end apart: 6 -> 7, of which waited for: 6 -> 7; matrix products, arithmetic and copies ran while one was open for 4% -> 6% of each run, Pallas kernels for 0% -> 0%
where the time goes in v1:
time: 761 us; the launch traced here: 760 us
  waiting for transfers between devices  682 us (90%)
  matrix products  23.4 us (3%)
  other arithmetic  20.7 us (3%)
  local copies, waits for them, and re-layouts  19.2 us (3%)
  between operations  14.4 us (2%)
    psum x1, waiting for transfers between devices, body(): lax.psum((jnp.dot(own_first.T, column_first, preferred_element_type=jnp.f...  265 us
    reduce_scatter x2, waiting for transfers between devices, ancestor_terms(): lax.psum_scatter(summed_terms(mirrored).astype(jnp.bfloat16), 'pcol', sca...  176 us
    all_gather x2, waiting for transfers between devices, from_root(): lax.all_gather(jnp.where(mine, shard, jnp.zeros_like(shard)), axis)  126 us
    all_gather x2, waiting for transfers between devices, ancestor_terms(): full = lax.all_gather(local, 'pcol', axis=1, tiled=True)  116 us
    unnamed x33, local copies, waits for them, and re-layouts  16.7 us
  transfers between devices with their start and end apart: 7, of which 7 were waited for; matrix products, arithmetic and copies ran while one was open for 6% of the time, Pallas kernels for 0%

profile of v1, /device:TPU:8, one launch (start us, length us, event | category | flops | bytes accessed | tf_op | source)
XLA Modules:
  0.0 760.4 jit_solution(15980895148990954117)
XLA Ops:
  7.2 0.0 copy-start
  7.2 0.0 all-gather.7.cloned.1.call-start
  7.2 0.8 fusion.13
  8.0 1.5 broadcast_multiply_fusion.1
  9.6 0.0 all-gather.7.cloned.1.call-update
  9.6 0.0 all-gather.9.cloned.1.call-start
  9.6 1.5 broadcast_multiply_fusion
  11.2 0.0 all-gather.9.cloned.1.call-update
  11.2 0.0 all-gather.11.cloned.1.call-start
  11.3 59.7 %all-gather.7.cloned.1.call-done = bf16[3072,512]{0,1:T(8,128)(2,1)} async-done(((bf16[3072,16]{0,1:T(8,128)(2,1)}), bf16[3072,512]{0,1:T(8,128)(2,1)}) %all-gather.7.cloned.1.call-update) | async-done | bytes 3145744 | tf_op jit(solution)/shard_map/all_gather | solution.py:60
  71.0 2.1 dynamic-slice_select_fusion.1
  73.2 0.0 all-gather.11.cloned.1.call-update
  73.2 0.0 all-gather.13.cloned.1.call-start
  73.2 55.8 %all-gather.9.cloned.1.call-done = bf16[3072,512]{0,1:T(8,128)(2,1)} async-done(((bf16[3072,16]{0,1:T(8,128)(2,1)}), bf16[3072,512]{0,1:T(8,128)(2,1)}) %all-gather.9.cloned.1.call-update) | async-done | bytes 3145744 | tf_op jit(solution)/shard_map/all_gather | solution.py:60
  129.0 2.1 dynamic-slice_select_fusion
  131.1 0.0 all-gather.13.cloned.1.call-update
  131.2 0.0 reduce-scatter.3.cloned.1.call-start
  131.2 0.8 dynamic-slice_convert_fusion.2
  132.0 2.5 mul.55
  134.5 0.0 slice-start.2
  134.5 2.9 copy.21
  137.5 64.4 %all-gather.11.cloned.1.call-done = bf16[6144,512]{0,1:T(8,128)(2,1)} async-done(((bf16[768,512]{0,1:T(8,128)(2,1)}), bf16[6144,512]{0,1:T(8,128)(2,1)}) %all-gather.11.cloned.1.call-update) | async-done | bytes 6291472 | tf_op jit(solution)/shard_map/all_gather | solution.py:11
  201.9 4.9 copy.22
  206.8 0.0 copy-start.1
  206.8 4.6 bitcast_reduce_fusion.1
  211.5 0.0 slice-done.2
  211.5 0.0 slice-done.3
  211.5 0.0 copy-done.1
  211.5 4.2 convolution_convert_fusion.1
  215.7 0.0 reduce-scatter.3.cloned.1.call-update
  215.7 0.2 reduce-scatter.5.cloned.1.call-start
  215.9 61.8 %all-gather.13.cloned.1.call-done = bf16[6144,512]{0,1:T(8,128)(2,1)} async-done(((bf16[768,512]{0,1:T(8,128)(2,1)}), bf16[6144,512]{0,1:T(8,128)(2,1)}) %all-gather.13.cloned.1.call-update) | async-done | bytes 6291472 | tf_op jit(solution)/shard_map/all_gather | solution.py:11
  277.7 4.9 copy.23
  282.7 4.6 bitcast_reduce_fusion
  287.3 0.0 slice-done
  287.3 0.0 slice-done.1
  287.4 6.4 convolution_convert_fusion
  293.8 0.0 reduce-scatter.5.cloned.1.call-update
  293.8 0.0 copy-start.7
  293.8 0.0 all-reduce.3.cloned.1.call-start
  293.9 84.1 %reduce-scatter.3.cloned.1.call-done = bf16[96,512]{1,0:T(8,128)(2,1)} async-done(((bf16[3072,512]{1,0:T(8,128)(2,1)}), bf16[96,512]{1,0:T(8,128)(2,1)}) %reduce-scatter.3.cloned.1.call-update) | async-done | bytes 98320 | tf_op jit(solution)/shard_map/reduce_scatter | solution.py:64
  378.0 0.9 negate_convert_fusion
  378.9 0.0 copy-start.5
  378.9 0.0 copy-start.6
  378.9 2.4 fusion.7
  381.3 2.3 fusion.11
  383.6 91.7 %reduce-scatter.5.cloned.1.call-done = bf16[96,512]{1,0:T(8,128)(2,1)} async-done(((bf16[3072,512]{1,0:T(8,128)(2,1)}), bf16[96,512]{1,0:T(8,128)(2,1)}) %reduce-scatter.5.cloned.1.call-update) | async-done | bytes 98320 | tf_op jit(solution)/shard_map/reduce_scatter | solution.py:64
  475.3 0.0 copy-done
  475.3 1.1 fusion.6
  476.4 0.0 copy-start.9
  476.4 2.4 fusion.9
  478.7 0.0 all-reduce.3.cloned.1.call-update
  478.8 0.0 copy-done.7
  478.8 1.3 copy.17
  480.1 264.6 %all-reduce.3.cloned.1.call-done = (f32[512,512]{1,0:T(8,128)}, f32[512,512]{1,0:T(8,128)}, f32[512,512]{0,1:T(8,128)}) async-done(((f32[512,512]{1,0:T(8,128)}, f32[512,512]{1,0:T(8,128)}, f32[512,512]{0,1:T(8,128)}), (f32[512,512]{1,0:T(8,128)}, f32[512,512]{1,0:T(8,128)}, f32[512,512]{0,1:T(8,128)})) %all-reduce.3.cloned.1.call-update) | async-done | bytes 3145744 | tf_op jit(solution)/shard_map/psum | solution.py:74
  744.7 1.6 sub.18
  746.3 0.0 copy-start.2
  746.3 2.6 fusion.2
  748.9 0.0 copy-start.3
  748.9 0.0 copy-done.4
  748.9 0.0 copy-done.8
  749.0 2.1 fusion.4
  751.0 2.5 copy.19
  753.5 0.0 copy-done.2
  (11 shorter events, 0.0 us)
Async XLA Ops:
  7.2 468.1 %copy-start = (bf16[512,512]{1,0:T(8,128)(2,1)S(1)}, bf16[512,512]{1,0:T(8,128)(2,1)}, u32[]{:S(2)}) copy-start(bf16[512,512]{1,0:T(8,128)(2,1)} %param.15) | copy-start | bytes 1572868
  7.2 63.8 %all-gather.7.cloned.1.call-start = ((), (), s32[]{:S(2)}) async-start(), calls=%async_computation.2 | async-start | bytes 3244032 | tf_op jit(solution)/shard_map/all_gather | solution.py:60
  9.6 119.4 %all-gather.9.cloned.1.call-start = ((), (), s32[]{:S(2)}) async-start(), calls=%async_computation.4 | async-start | bytes 3244032 | tf_op jit(solution)/shard_map/all_gather | solution.py:60
  11.2 190.7 %all-gather.11.cloned.1.call-start = ((), (), s32[]{:S(2)}) async-start(), calls=%async_computation.6 | async-start | bytes 7077888 | tf_op jit(solution)/shard_map/all_gather | solution.py:11
  73.2 204.5 %all-gather.13.cloned.1.call-start = ((), (), s32[]{:S(2)}) async-start(), calls=%async_computation.7 | async-start | bytes 7077888 | tf_op jit(solution)/shard_map/all_gather | solution.py:11
  131.2 246.8 %reduce-scatter.3.cloned.1.call-start = ((), (), s32[]{:S(2)}) async-start(), calls=%async_computation.3 | async-start | bytes 3244032 | tf_op jit(solution)/shard_map/reduce_scatter | solution.py:64
  134.5 77.0 %slice-start.2 = ((s8[4718592]{0:T(1024)(128)(4,1)}), s8[524288]{0:T(1024)(128)(4,1)S(1)}, s32[]{:S(2)}) async-start(s8[4718592]{0:T(1024)(128)(4,1)} %bitcast.37), calls=%async_computation.11 | async-start | bytes 1048576
  201.9 9.6 %slice-start.3 = ((s8[4718592]{0:T(1024)(128)(4,1)}), s8[4194304]{0:T(1024)(128)(4,1)S(1)}, s32[]{:S(2)}) async-start(s8[4718592]{0:T(1024)(128)(4,1)} %bitcast.37), calls=%async_computation.12 | async-start | bytes 8388608
  206.8 4.7 copy-start.1
  215.7 71.7 %slice-start = ((s8[4718592]{0:T(1024)(128)(4,1)}), s8[524288]{0:T(1024)(128)(4,1)S(1)}, s32[]{:S(2)}) async-start(s8[4718592]{0:T(1024)(128)(4,1)} %bitcast.34), calls=%async_computation.9 | async-start | bytes 1048576
  215.7 259.6 %reduce-scatter.5.cloned.1.call-start = ((), (), s32[]{:S(2)}) async-start(), calls=%async_computation.5 | async-start | bytes 3244032 | tf_op jit(solution)/shard_map/reduce_scatter | solution.py:64
  277.7 9.6 %slice-start.1 = ((s8[4718592]{0:T(1024)(128)(4,1)}), s8[4194304]{0:T(1024)(128)(4,1)S(1)}, s32[]{:S(2)}) async-start(s8[4718592]{0:T(1024)(128)(4,1)} %bitcast.34), calls=%async_computation.10 | async-start | bytes 8388608
  293.8 184.9 %copy-start.7 = (f32[512,512]{1,0:T(8,128)S(1)}, f32[512,512]{1,0:T(8,128)}, u32[]{:S(2)}) copy-start(f32[512,512]{1,0:T(8,128)} %param.17) | copy-start | bytes 3145732
  293.8 450.9 %all-reduce.3.cloned.1.call-start = ((), (), s32[]{:S(2)}) async-start(), calls=%async_computation.8 | async-start | bytes 6291456 | tf_op jit(solution)/shard_map/psum | solution.py:74
  378.9 101.2 %copy-start.5 = (bf16[96,512]{1,0:T(8,128)(2,1)}, bf16[96,512]{1,0:T(8,128)(2,1)S(1)}, u32[]{:S(2)}) copy-start(bf16[96,512]{1,0:T(8,128)(2,1)S(1)} %negate_convert_fusion) | copy-start | bytes 294916
  378.9 365.8 %copy-start.6 = (f32[512,512]{1,0:T(8,128)S(1)}, f32[512,512]{1,0:T(8,128)}, u32[]{:S(2)}) copy-start(f32[512,512]{1,0:T(8,128)} %param.16) | copy-start | bytes 3145732
  476.4 269.9 %copy-start.9 = (bf16[96,512]{1,0:T(8,128)(2,1)}, bf16[96,512]{1,0:T(8,128)(2,1)S(1)}, u32[]{:S(2)}) copy-start(bf16[96,512]{1,0:T(8,128)(2,1)S(1)} %fusion.6) | copy-start | bytes 294916
  744.7 4.2 copy-start.4
  744.7 4.2 copy-start.8
  746.3 7.2 copy-start.2
  748.9 4.6 copy-start.3
Sparse Core Ops, SparseCore 0:
  11.1 59.8 all-gather.6
  74.1 54.8 all-gather.8
  131.4 70.4 all-gather.10
  204.1 73.6 all-gather.12
  281.5 96.4 reduce-scatter.2
  382.3 92.9 reduce-scatter.4
  481.6 263.0 all-reduce.2
